TPU v7x, 512 devices: a whole 4x4x16 slice. The times are simulated.
512 devices in a mesh: dp: 16 (over z), retr: 8 (over x, core), fsdp: 4 (over y).
Axes of the slice: x: 4, y: 4, z: 16, core: 2. Of those that a mesh axis runs over, the one named last changes fastest.
Arguments:
- queries: bfloat16 [65536, 2048], P(('dp', 'retr', 'fsdp')), may hold values from -110 to 110, as said below
- encodings: bfloat16 [2048, 128, 896], P(('dp', 'retr', 'fsdp')), may hold values from -6 to 6
- owner_ids: int32 [1024, 2], P(('dp', 'retr', 'fsdp')), may hold values from 0 to 7, all different within a row; in each aligned block of 2 rows (0 to 1, 2 to 3, ...) at most 2 rows name the same one
- local_ids: int32 [1024, 2], P(('dp', 'retr', 'fsdp')), may hold values from 0 to 3
- key_weight: bfloat16 [896, 2048], P(('dp', 'fsdp')), may hold values from -0.1875 to 0.1875
- value_weight: bfloat16 [896, 2048], P(('dp', 'fsdp')), may hold values from -0.1875 to 0.1875
Outputs:
- attended: bfloat16 [65536, 2048], P(('dp', 'retr', 'fsdp'))
Inputs may be any that keep to these rules, and one draw needn't show every extreme that they name: `queries`: entries are bounded. `owner_ids`: the two neighbours of a stretch have different owners; among the stretches of one device no owner is named more than 2 times, and in every draw some device's stretches name some owner exactly 2 times.
All inputs are finite; a program needn't handle non-finite values.
Results may differ from a plain program's by a relative error of at most 0.011.
Values may be sent and summed in bfloat16 or wider, within the bound.
No kernel may reach another device: no remote copies, remote signals or barrier semaphores. Data moves between devices by JAX's collectives and lax.ppermute only.
A program may use at most 64 MiB of HBM per device.

v0:
```python
import math

import jax
import jax.numpy as jnp
from jax import lax
from jax.sharding import PartitionSpec as P

HEADS = 16
STRETCH = 64


def passed_along(block, axis, distance):
    devices = range(lax.axis_size(axis))
    route = [(i - distance, i) for i in devices if i - distance in devices]
    return lax.ppermute(block, axis, route)


def body(queries, encodings, owner_ids, local_ids, key_weight, value_weight):
    tokens = queries.shape[0]
    columns = queries.shape[1]
    head_size = columns // HEADS
    stretches = tokens // STRETCH
    neighbours = owner_ids.shape[1]
    slot_count = stretches * neighbours
    owners = owner_ids.reshape(slot_count)
    places = local_ids.reshape(slot_count)
    gathered = lax.all_gather(encodings, "retr", axis=0, tiled=True)
    fetched = jnp.take(gathered, owners * encodings.shape[0] + places, axis=0)
    span = neighbours * encodings.shape[1]
    panel_rows = fetched.reshape(stretches * span, encodings.shape[2])
    key_full, value_full = (
        lax.all_gather(key_weight, ("dp", "fsdp"), axis=0, tiled=True),
        lax.all_gather(value_weight, ("dp", "fsdp"), axis=0, tiled=True),
    )
    prior_rows = passed_along(panel_rows[(stretches - 1) * span :], "fsdp", 1)
    every_row = jnp.concatenate([prior_rows, panel_rows], 0)
    key_block = jnp.dot(every_row, key_full, preferred_element_type=jnp.float32).astype(
        jnp.bfloat16
    )
    value_block = jnp.dot(every_row, value_full, preferred_element_type=jnp.float32).astype(
        jnp.bfloat16
    )
    key_block = key_block.reshape(stretches + 1, span, columns)
    value_block = value_block.reshape(stretches + 1, span, columns)
    padded = jnp.concatenate(
        [
            jnp.zeros((1, columns), jnp.bfloat16),
            queries,
            jnp.zeros((STRETCH - 1, columns), jnp.bfloat16),
        ],
        0,
    )
    query_block = padded.reshape(stretches + 1, STRETCH, HEADS, head_size)
    key_heads = key_block.reshape(stretches + 1, span, HEADS, head_size)
    value_heads = value_block.reshape(stretches + 1, span, HEADS, head_size)
    scores = jnp.einsum(
        "cqhd,ckhd->chqk", query_block, key_heads, preferred_element_type=jnp.float32
    ) / math.sqrt(head_size)
    probs = jax.nn.softmax(scores, axis=-1).astype(jnp.bfloat16)
    result = jnp.einsum(
        "chqk,ckhd->cqhd", probs, value_heads, preferred_element_type=jnp.float32
    ).astype(jnp.bfloat16)
    result = result.reshape((stretches + 1) * STRETCH, columns)[1 : tokens + 1]
    follower = lax.axis_index("fsdp") > 0
    position = jnp.arange(tokens, dtype=jnp.int32)
    visible = follower | (position >= STRETCH - 1)
    return jnp.where(visible[:, None], result, jnp.zeros_like(result))


def solution(mesh):
    in_specs = (
        P(("dp", "retr", "fsdp"), None),
        P(("dp", "retr", "fsdp"), None, None),
        P(("dp", "retr", "fsdp"), None),
        P(("dp", "retr", "fsdp"), None),
        P(("dp", "fsdp"), None),
        P(("dp", "fsdp"), None),
    )
    out_specs = P(("dp", "retr", "fsdp"), None)
    return jax.shard_map(body, mesh=mesh, in_specs=in_specs, out_specs=out_specs, check_vma=False)
```

profile of v0, /device:TPU:2, one launch (start us, length us, event | category | flops | bytes accessed | tf_op | source)
XLA Modules:
  0.0 400.2 jit_solution(17860496296428153999)
XLA Ops:
  6.5 0.7 all-gather.6.cloned.1.call-update
  7.3 0.7 all-gather.8.cloned.1.call-update
  8.0 0.0 all-gather.10.cloned.1.call-start
  8.1 0.7 all-gather.10.cloned.1.call-update
  8.7 0.7 multiply_add_fusion
  9.4 0.1 add.36
  9.5 0.1 add.34
  9.6 0.1 slice.14
  9.7 0.1 pad.4.clone
  9.8 1.4 maximum_bitcast_fusion
  11.2 1.1 copy.17
  12.3 53.7 %all-gather.6.cloned.1.call-done = bf16[32,128,896]{2,1,0:T(8,128)(2,1)} async-done(((bf16[4,128,896]{2,1,0:T(8,128)(2,1)}), bf16[32,128,896]{2,1,0:T(8,128)(2,1)}) %all-gather.6.cloned.1.call-update) | async-done | bytes 7340048 | tf_op jit(solution)/shard_map/all_gather | solution.py:27
  66.0 3.8 gather_fusion
  69.8 0.1 slice_select_fusion.1
  69.9 3.4 collective-permute-start
  73.3 0.1 broadcast_bitcast_fusion
  73.4 142.8 %all-gather.8.cloned.1.call-done = bf16[64,14,2048]{2,1,0:T(8,128)(2,1)} async-done(((bf16[1,14,2048]{2,1,0:T(8,128)(2,1)}), bf16[64,14,2048]{2,1,0:T(8,128)(2,1)}) %all-gather.8.cloned.1.call-update) | async-done | bytes 3670032 | tf_op jit(solution)/shard_map/all_gather | solution.py:33
  216.3 6.0 %reshape.73 = bf16[896,2048]{1,0:T(8,128)(2,1)} reshape(bf16[64,14,2048]{2,1,0:T(8,128)(2,1)} %all-gather.8.cloned.1.call-done) | data formatting | bytes 7340032
  222.2 137.9 %all-gather.10.cloned.1.call-done = bf16[64,14,2048]{2,1,0:T(8,128)(2,1)} async-done(((bf16[1,14,2048]{2,1,0:T(8,128)(2,1)}), bf16[64,14,2048]{2,1,0:T(8,128)(2,1)}) %all-gather.10.cloned.1.call-update) | async-done | bytes 3670032 | tf_op jit(solution)/shard_map/all_gather | solution.py:32
  360.1 6.0 %reshape.75 = bf16[896,2048]{1,0:T(8,128)(2,1)} reshape(bf16[64,14,2048]{2,1,0:T(8,128)(2,1)} %all-gather.10.cloned.1.call-done) | data formatting | bytes 7340032
  366.2 0.2 bitcast_select_fusion
  366.4 6.0 %fusion.8 = bf16[96,8,16,128]{3,1,2,0:T(8,128)(2,1)S(1)} fusion(bf16[896,2048]{1,0:T(8,128)(2,1)} %reshape.73, bf16[512,896]{1,0:T(8,128)(2,1)S(1)} %bitcast_select_fusion, bf16[256,896]{1,0:T(8,128)(2,1)S(1)} %collective-permute-done), kind=kOutput, calls=%fused_computation.12 | convolution fusion | flops 2822897664 | bytes 8192000 | tf_op jit(solution)/shard_map/dot_general | solution.py:40
  372.5 2.7 copy.19
  375.2 4.0 fusion.9
  379.1 1.0 copy.18
  380.2 0.1 copy-done.1
  380.3 1.2 fusion.3
  381.5 1.1 fusion.30
  382.6 8.2 %fusion.15 = bf16[3,64,16,128]{3,1,2,0:T(8,128)(2,1)} fusion(bf16[3,256,16,128]{3,2,1,0:T(8,128)(2,1)} %bitcast.33, f32[3,16,64]{2,1,0:T(8,128)S(1)} %fusion.30, f32[3,16,64,256]{3,2,1,0:T(8,128)S(1)} %fusion.3), kind=kOutput, calls=%fused_computation.18 | convolution fusion | flops 205655296 | bytes 7090176 | tf_op jit(solution)/shard_map/chqk,ckhd->cqhd/dot_general | solution.py:60
  390.9 1.6 copy.16
  392.5 0.2 copy.32
  392.7 1.0 slice_select_fusion
  (12 shorter events, 0.1 us)
Async XLA Ops:
  6.5 59.5 %all-gather.6.cloned.1.call-start = ((), (), s32[]{:S(2)}) async-start(), calls=%async_computation | async-start | bytes 8257536 | tf_op jit(solution)/shard_map/all_gather | solution.py:27
  7.3 209.0 %all-gather.8.cloned.1.call-start = ((), (), s32[]{:S(2)}) async-start(), calls=%async_computation.1 | async-start | bytes 4259840 | tf_op jit(solution)/shard_map/all_gather | solution.py:33
  8.0 352.1 %all-gather.10.cloned.1.call-start = ((), (), s32[]{:S(2)}) async-start(), calls=%async_computation.2 | async-start | bytes 4259840 | tf_op jit(solution)/shard_map/all_gather | solution.py:32
  69.9 296.5 %collective-permute-start = (bf16[256,896]{1,0:T(8,128)(2,1)S(1)}, bf16[256,896]{1,0:T(8,128)(2,1)S(1)}, u32[]{:S(2)}, u32[]{:S(2)}) collective-permute-start(bf16[256,896]{1,0:T(8,128)(2,1)S(1)} %bitcast.36), channel_id=1, source_target_pairs={{0,1},{1,2},{2,3},{4,5},{5,6},{6,7},{8,9},{9,10},{10,11},{12,13},{... | collective-permute-start | bytes 1376264 | tf_op jit(solution)/shard_map/ppermute | solution.py:15
  372.5 2.7 copy-start
  379.1 1.1 copy-start.1
Sparse Core Ops, SparseCore 0:
  9.5 56.5 all-gather.5
  68.9 147.2 all-gather.7
  219.2 140.8 all-gather.9
where the time goes:
time: 401 us; the launch traced here: 400 us
  waiting for transfers between devices  337 us (84%)
  local copies, waits for them, and re-layouts  22.9 us (6%)
  matrix products  19.5 us (5%)
  between operations  13.2 us (3%)
  other arithmetic  4.63 us (1%)
    all_gather x1, waiting for transfers between devices, body(): lax.all_gather(value_weight, ('dp', 'fsdp'), axis=0, tiled=True)  143 us
    all_gather x1, waiting for transfers between devices, body(): lax.all_gather(key_weight, ('dp', 'fsdp'), axis=0, tiled=True)  138 us
    all_gather x1, waiting for transfers between devices, body(): gathered = lax.all_gather(encodings, 'retr', axis=0, tiled=True)  53.7 us
    unnamed x10, local copies, waits for them, and re-layouts  17.1 us
    dot_general x1, matrix products, body(): jnp.einsum('chqk,ckhd->cqhd', probs, value_heads, preferred_element_type=...  8.23 us
  transfers between devices with their start and end apart: 4, of which 3 were waited for; matrix products, arithmetic and copies ran while one was open for 5% of the time, Pallas kernels for 0%

commit v1 on v0

v1 whole, which is shorter than its diff:
```python
import functools
import math

import jax
import jax.numpy as jnp
from jax import lax
from jax.experimental import pallas as pl
from jax.experimental.pallas import tpu as pltpu
from jax.sharding import PartitionSpec as P

HEADS = 16
STRETCH = 64


def attend_kernel(ids_ref, q_ref, kv_ref, o_ref, *, heads, head_size, stretches, neighbours, scale):
    source = pl.program_id(0)
    columns = heads * head_size
    for j in range(stretches):
        base = (source * stretches + j) * neighbours
        panels = [ids_ref[base + n] for n in range(neighbours)]
        for h in range(heads):
            low = h * head_size
            k = jnp.concatenate([kv_ref[p, :, low : low + head_size] for p in panels], 0)
            v = jnp.concatenate(
                [kv_ref[p, :, columns + low : columns + low + head_size] for p in panels], 0
            )
            q = q_ref[0, j * STRETCH : (j + 1) * STRETCH, low : low + head_size]
            s = (
                lax.dot_general(
                    q, k, (((1,), (1,)), ((), ())), preferred_element_type=jnp.float32
                )
                * scale
            )
            e = jnp.exp(s - jnp.max(s, axis=-1, keepdims=True))
            probs = (e * (1.0 / jnp.sum(e, axis=-1, keepdims=True))).astype(jnp.bfloat16)
            out = jnp.dot(probs, v, preferred_element_type=jnp.float32)
            o_ref[0, j * STRETCH : (j + 1) * STRETCH, low : low + head_size] = out.astype(
                jnp.bfloat16
            )


def spread(block, axis):
    size = lax.axis_size(axis)
    return lax.all_to_all(jnp.broadcast_to(block[None], (size, *block.shape)), axis, 0, 0)


def body(queries, encodings, owner_ids, local_ids, key_weight, value_weight):
    tokens, columns = queries.shape
    stretches = tokens // STRETCH
    neighbours = owner_ids.shape[1]
    group = lax.axis_size("retr")
    mine = columns // group
    head_size = columns // HEADS
    panels = encodings.shape[0]
    width = encodings.shape[2]
    rank = lax.axis_index("retr")
    followers = [(i, i + 1) for i in range(lax.axis_size("fsdp") - 1)]
    leaders = [(i + 1, i) for i in range(lax.axis_size("fsdp") - 1)]

    cut = jnp.concatenate(
        [
            lax.dynamic_slice_in_dim(key_weight, rank * mine, mine, 1),
            lax.dynamic_slice_in_dim(value_weight, rank * mine, mine, 1),
        ],
        1,
    )
    by_dp = spread(cut, "dp")
    by_all = spread(by_dp, "fsdp")
    weight = by_all.transpose(1, 0, 2, 3).reshape(width, 2 * mine)

    late = lax.ppermute(queries[:STRETCH], "fsdp", leaders)
    shifted = jnp.concatenate([queries[STRETCH - 1 :], late[: STRETCH - 1]], 0)
    slots = (owner_ids * panels + local_ids).astype(jnp.bfloat16).reshape(1, 1, stretches * neighbours)
    notes = jnp.pad(
        jnp.broadcast_to(slots, (group, 1, stretches * neighbours)),
        ((0, 0), (0, 15), (0, mine - stretches * neighbours)),
    )
    blocks = shifted.reshape(tokens, group, mine).transpose(1, 0, 2)
    swapped = lax.all_to_all(jnp.concatenate([blocks, notes], 1), "retr", 0, 0)
    ids = swapped[:, tokens, : stretches * neighbours].astype(jnp.int32).reshape(-1)

    everyone = lax.all_gather(encodings, "retr", axis=0, tiled=True)
    kv = jnp.dot(
        everyone.reshape(-1, width), weight, preferred_element_type=jnp.float32
    ).astype(jnp.bfloat16)
    kv = kv.reshape(everyone.shape[0], everyone.shape[1], 2 * mine)

    attended = pl.pallas_call(
        functools.partial(
            attend_kernel,
            heads=mine // head_size,
            head_size=head_size,
            stretches=stretches,
            neighbours=neighbours,
            scale=1.0 / math.sqrt(head_size),
        ),
        out_shape=jax.ShapeDtypeStruct((group, tokens, mine), jnp.bfloat16),
        grid_spec=pltpu.PrefetchScalarGridSpec(
            num_scalar_prefetch=1,
            grid=(group,),
            in_specs=[
                pl.BlockSpec((1, tokens, mine), lambda g, ids: (g, 0, 0)),
                pl.BlockSpec(kv.shape, lambda g, ids: (0, 0, 0)),
            ],
            out_specs=pl.BlockSpec((1, tokens, mine), lambda g, ids: (g, 0, 0)),
        ),
    )(ids, swapped, kv)

    split = tokens - STRETCH
    ahead = lax.ppermute(attended[:, split:], "fsdp", followers)
    ordered = jnp.concatenate([ahead[:, 1:], attended[:, : split + 1]], 1)
    back = lax.all_to_all(ordered, "retr", 0, 0)
    return back.transpose(1, 0, 2).reshape(tokens, columns)


def solution(mesh):
    in_specs = (
        P(("dp", "retr", "fsdp"), None),
        P(("dp", "retr", "fsdp"), None, None),
        P(("dp", "retr", "fsdp"), None),
        P(("dp", "retr", "fsdp"), None),
        P(("dp", "fsdp"), None),
        P(("dp", "fsdp"), None),
    )
    out_specs = P(("dp", "retr", "fsdp"), None)
    return jax.shard_map(body, mesh=mesh, in_specs=in_specs, out_specs=out_specs, check_vma=False)
```

time: 401 us -> 145 us (0.36)
  the two profiles are of different devices: /device:TPU:2 before, /device:TPU:8 now
where the time goes in v1:
time: 145 us
  waiting for transfers between devices  47.3 us (33%)
  starting transfers between devices  28.7 us (20%)
  local copies, waits for them, and re-layouts  16.9 us (12%)
  Pallas kernels  15 us (10%)
  between operations  13.5 us (9%)
  blocking collectives  12.8 us (9%)
  matrix products  9.3 us (6%)
    all_to_all x2, starting transfers between devices, spread(): lax.all_to_all(jnp.broadcast_to(block[None], (size, *block.shape)), axis,...  20.1 us
    all_to_all x1, waiting for transfers between devices, body(): swapped = lax.all_to_all(jnp.concatenate([blocks, notes], 1), 'retr', 0, 0)  17.6 us
    pallas_call x1, Pallas kernels, body(): pl.pallas_call(functools.partial(attend_kernel, heads=mine // head_size,...  15 us
    all_to_all x1, blocking collectives, body(): back = lax.all_to_all(ordered, 'retr', 0, 0)  12.8 us
    all_to_all x2, waiting for transfers between devices, spread(): lax.all_to_all(jnp.broadcast_to(block[None], (size, *block.shape)), axis,...  11.8 us
    ppermute x1, waiting for transfers between devices, body(): late = lax.ppermute(queries[:STRETCH], 'fsdp', leaders)  11.4 us
    dot_general x1, matrix products, body(): jnp.dot(everyone.reshape(-1, width), weight, preferred_element_type=jnp.f...  9.3 us
    convert_element_type x1, local copies, waits for them, and re-layouts, body(): kv = jnp.dot(everyone.reshape(-1, width), weight, preferred_element_type=...  6.48 us
  transfers between devices with their start and end apart: 6, of which 5 were waited for; matrix products, arithmetic and copies ran while one was open for 6% of the time, Pallas kernels for 0%

profile of v1, /device:TPU:8, one launch (start us, length us, event | category | flops | bytes accessed | tf_op | source)
XLA Modules:
  0.0 144.7 jit_solution(9525122055811373839)
XLA Ops:
  6.5 0.7 all-gather.2.cloned.1.call-update
  7.3 0.7 constant_dynamic-slice_fusion
  8.0 0.7 broadcast_in_dim.7
  8.7 15.2 %all-to-all-start.1 = ((bf16[16,14,512]{2,1,0:T(8,128)(2,1)}), bf16[16,14,512]{2,1,0:T(8,128)(2,1)S(1)}, u32[]{:S(2)}, u32[]{:S(2)}) async-start(bf16[16,14,512]{2,1,0:T(8,128)(2,1)} %broadcast_in_dim.7), calls=%async_computation.1 | async-start | bytes 524288 | tf_op jit(solution)/shard_map/all_to_all | solution.py:44
  23.9 1.0 slice.22
  24.9 0.3 copy.30
  25.2 2.4 %collective-permute-start = (bf16[64,2048]{0,1:T(8,128)(2,1)S(1)}, bf16[64,2048]{0,1:T(8,128)(2,1)S(1)}, u32[]{:S(2)}, u32[]{:S(2)}) collective-permute-start(bf16[64,2048]{0,1:T(8,128)(2,1)S(1)} %copy.30), channel_id=1, source_target_pairs={{1,0},{2,1},{3,2},{5,4},{6,5},{7,6},{9,8},{10,9},{11,10},{13,12},{... | collective-permute-start | bytes 786440 | tf_op jit(solution)/shard_map/ppermute | solution.py:71
  27.5 1.0 slice.21
  28.6 0.3 copy.29
  29.0 11.4 %collective-permute-done = bf16[64,2048]{0,1:T(8,128)(2,1)S(1)} collective-permute-done((bf16[64,2048]{0,1:T(8,128)(2,1)S(1)}, bf16[64,2048]{0,1:T(8,128)(2,1)S(1)}, u32[]{:S(2)}, u32[]{:S(2)}) %collective-permute-start) | collective-permute-done | bytes 262176 | tf_op jit(solution)/shard_map/ppermute | solution.py:71
  40.5 0.3 pad_maximum_fusion.1
  40.8 0.2 copy.23
  41.0 0.9 pad_maximum_fusion
  41.9 0.5 all-to-all-done.1
  42.3 4.3 %all-to-all-start = ((bf16[8,144,256]{2,1,0:T(8,128)(2,1)}), bf16[8,144,256]{2,1,0:T(8,128)(2,1)S(1)}, u32[]{:S(2)}, u32[]{:S(2)}) async-start(bf16[8,144,256]{2,1,0:T(8,128)(2,1)} %pad_maximum_fusion), calls=%async_computation | async-start | bytes 1179648 | tf_op jit(solution)/shard_map/all_to_all | solution.py:79
  46.7 17.6 %all-to-all-done.q_ref = bf16[8,144,256]{2,1,0:T(8,128)(2,1)S(1)} async-done(((bf16[8,144,256]{2,1,0:T(8,128)(2,1)}), bf16[8,144,256]{2,1,0:T(8,128)(2,1)S(1)}, u32[]{:S(2)}, u32[]{:S(2)}) %all-to-all-start) | async-done | bytes 589856 | tf_op jit(solution)/shard_map/all_to_all | solution.py:79
  64.4 1.1 broadcast_in_dim.8
  65.5 4.9 %all-to-all-start.2 = ((bf16[4,16,14,512]{3,1,2,0:T(8,128)(2,1)}), bf16[4,16,14,512]{3,1,2,0:T(8,128)(2,1)S(1)}, u32[]{:S(2)}, u32[]{:S(2)}) async-start(bf16[4,16,14,512]{3,1,2,0:T(8,128)(2,1)} %broadcast_in_dim.8), calls=%async_computation.2 | async-start | bytes 1835008 | tf_op jit(solution)/shard_map/all_to_all | solution.py:44
  70.4 0.7 reshape.32.ids_ref
  71.1 11.4 %all-to-all-done.2 = bf16[4,16,14,512]{3,1,2,0:T(8,128)(2,1)S(1)} async-done(((bf16[4,16,14,512]{3,1,2,0:T(8,128)(2,1)}), bf16[4,16,14,512]{3,1,2,0:T(8,128)(2,1)S(1)}, u32[]{:S(2)}, u32[]{:S(2)}) %all-to-all-start.2) | async-done | bytes 917536 | tf_op jit(solution)/shard_map/all_to_all | solution.py:44
  82.5 0.5 copy.25
  83.0 0.3 reshape.28
  83.3 9.3 %fusion = bf16[4096,512]{0,1:T(8,128)(2,1)} fusion(bf16[896,512]{1,0:T(8,128)(2,1)S(1)} %reshape.28, bf16[4096,896]{1,0:T(8,128)(2,1)} %bitcast.19), kind=kOutput, calls=%fused_computation.1 | convolution fusion | flops 3760193536 | bytes 12451840 | tf_op jit(solution)/shard_map/dot_general | solution.py:83
  92.6 6.5 %copy.26 = bf16[4096,512]{1,0:T(8,128)(2,1)} copy(bf16[4096,512]{0,1:T(8,128)(2,1)} %fusion) | data formatting | bytes 8388608 | tf_op jit(solution)/shard_map/convert_element_type | solution.py:85
  99.1 15.0 %shard_map.64 = bf16[8,128,256]{2,1,0:T(8,128)(2,1)} custom-call(s32[32]{0:T(128)} %reshape.32.ids_ref, bf16[8,144,256]{2,1,0:T(8,128)(2,1)} %copy-done, bf16[32,128,512]{2,1,0:T(8,128)(2,1)} %bitcast.12), custom_call_target="tpu_custom_call" | custom-call | tf_op jit(solution)/shard_map/pallas_call | solution.py:88
  114.0 1.0 slice.30
  115.0 1.9 %collective-permute-start.1 = (bf16[8,64,256]{2,1,0:T(8,128)(2,1)S(1)}, bf16[8,64,256]{2,1,0:T(8,128)(2,1)S(1)}, u32[]{:S(2)}, u32[]{:S(2)}) collective-permute-start(bf16[8,64,256]{2,1,0:T(8,128)(2,1)S(1)} %slice.30), channel_id=1, source_target_pairs={{0,1},{1,2},{2,3},{4,5},{5,6},{6,7},{8,9},{9,10},{10,11},{12,13},{... | collective-permute-start | bytes 786440 | tf_op jit(solution)/shard_map/ppermute | solution.py:110
  116.9 1.0 slice.32
  117.9 5.7 %collective-permute-done.1 = bf16[8,64,256]{2,1,0:T(8,128)(2,1)S(1)} collective-permute-done((bf16[8,64,256]{2,1,0:T(8,128)(2,1)S(1)}, bf16[8,64,256]{2,1,0:T(8,128)(2,1)S(1)}, u32[]{:S(2)}, u32[]{:S(2)}) %collective-permute-start.1) | collective-permute-done | bytes 262176 | tf_op jit(solution)/shard_map/ppermute | solution.py:110
  123.8 12.8 %all_to_all.20 = bf16[8,128,256]{2,1,0:T(8,128)(2,1)S(1)} all-to-all(bf16[8,128,256]{2,1,0:T(8,128)(2,1)S(1)} %pad_maximum_fusion.2), channel_id=1, replica_groups=mesh['dp'=16,'retr'=8,'fsdp'=4] {'retr'}, dimensions={0} | all-to-all | bytes 1048576 | tf_op jit(solution)/shard_map/all_to_all | solution.py:112
  136.6 0.3 copy.27
  136.8 1.0 copy.28
  (17 shorter events, 0.5 us)
Async XLA Ops:
  6.5 22.4 %copy-start.2 = (s32[2,2]{1,0:T(2,128)S(1)}, s32[2,2]{1,0:T(2,128)}, u32[]{:S(2)}) copy-start(s32[2,2]{1,0:T(2,128)} %param.8) | copy-start | bytes 52
  6.5 22.4 %copy-start.1 = (s32[2,2]{1,0:T(2,128)S(1)}, s32[2,2]{1,0:T(2,128)}, u32[]{:S(2)}) copy-start(s32[2,2]{1,0:T(2,128)} %param.9) | copy-start | bytes 52
  6.5 76.7 %all-gather.2.cloned.1.call-start = ((), (), s32[]{:S(2)}) async-start(), calls=%async_computation.4 | async-start | bytes 8257536 | tf_op jit(solution)/shard_map/all_gather | solution.py:82
  8.7 33.6 %all-to-all-start.1 = ((bf16[16,14,512]{2,1,0:T(8,128)(2,1)}), bf16[16,14,512]{2,1,0:T(8,128)(2,1)S(1)}, u32[]{:S(2)}, u32[]{:S(2)}) async-start(bf16[16,14,512]{2,1,0:T(8,128)(2,1)} %broadcast_in_dim.7), calls=%async_computation.1 | async-start | bytes 524288 | tf_op jit(solution)/shard_map/all_to_all | solution.py:44
  25.2 15.3 %collective-permute-start = (bf16[64,2048]{0,1:T(8,128)(2,1)S(1)}, bf16[64,2048]{0,1:T(8,128)(2,1)S(1)}, u32[]{:S(2)}, u32[]{:S(2)}) collective-permute-start(bf16[64,2048]{0,1:T(8,128)(2,1)S(1)} %copy.30), channel_id=1, source_target_pairs={{1,0},{2,1},{3,2},{5,4},{6,5},{7,6},{9,8},{10,9},{11,10},{13,12},{... | collective-permute-start | bytes 786440 | tf_op jit(solution)/shard_map/ppermute | solution.py:71
  42.3 22.1 %all-to-all-start = ((bf16[8,144,256]{2,1,0:T(8,128)(2,1)}), bf16[8,144,256]{2,1,0:T(8,128)(2,1)S(1)}, u32[]{:S(2)}, u32[]{:S(2)}) async-start(bf16[8,144,256]{2,1,0:T(8,128)(2,1)} %pad_maximum_fusion), calls=%async_computation | async-start | bytes 1179648 | tf_op jit(solution)/shard_map/all_to_all | solution.py:79
  64.4 28.2 %copy-start = (bf16[8,144,256]{2,1,0:T(8,128)(2,1)}, bf16[8,144,256]{2,1,0:T(8,128)(2,1)S(1)}, u32[]{:S(2)}) copy-start(bf16[8,144,256]{2,1,0:T(8,128)(2,1)S(1)} %all-to-all-done.q_ref) | copy-start | bytes 1769476
  65.5 17.0 %all-to-all-start.2 = ((bf16[4,16,14,512]{3,1,2,0:T(8,128)(2,1)}), bf16[4,16,14,512]{3,1,2,0:T(8,128)(2,1)S(1)}, u32[]{:S(2)}, u32[]{:S(2)}) async-start(bf16[4,16,14,512]{3,1,2,0:T(8,128)(2,1)} %broadcast_in_dim.8), calls=%async_computation.2 | async-start | bytes 1835008 | tf_op jit(solution)/shard_map/all_to_all | solution.py:44
  115.0 8.6 %collective-permute-start.1 = (bf16[8,64,256]{2,1,0:T(8,128)(2,1)S(1)}, bf16[8,64,256]{2,1,0:T(8,128)(2,1)S(1)}, u32[]{:S(2)}, u32[]{:S(2)}) collective-permute-start(bf16[8,64,256]{2,1,0:T(8,128)(2,1)S(1)} %slice.30), channel_id=1, source_target_pairs={{0,1},{1,2},{2,3},{4,5},{5,6},{6,7},{8,9},{9,10},{10,11},{12,13},{... | collective-permute-start | bytes 786440 | tf_op jit(solution)/shard_map/ppermute | solution.py:110
Sparse Core Ops, SparseCore 0:
  9.5 63.5 all-gather.1
